TPU v7x, 32 devices: a whole 2x2x4 slice. The times are simulated.
32 devices in a mesh: seq: 8 (over y, x, core), tile: 4 (over z).
Axes of the slice: x: 2, y: 2, z: 4, core: 2. Of those that a mesh axis runs over, the one named last changes fastest.
Arguments:
- inputs: bfloat16 [8, 13, 256, 1024], P('seq', None, 'tile'), may hold values from -6 to 6
- actions: int32 [8, 13], P('seq'), may hold values from 0 to 7
- segments: int32 [8, 13], P('seq'), may hold values from 0 to 3, never falling along the last dimension, each value on 1 to 6 neighbouring positions
- cotangent: bfloat16 [8, 13, 256, 1024], P('seq', None, 'tile'), may hold values from -6 to 6
- action_table: bfloat16 [8, 1024], P(None, 'seq'), may hold values from -6 to 6
- spatial_inward: bfloat16 [1024, 3072], P('seq'), may hold values from -0.1875 to 0.1875
- spatial_outward: bfloat16 [1024, 1024], P('seq'), may hold values from -3 to 3
- temporal_inward: bfloat16 [1024, 3072], P('seq'), may hold values from -0.1875 to 0.1875
- temporal_outward: bfloat16 [1024, 1024], P('seq'), may hold values from -0.375 to 0.375
- expand_weight: bfloat16 [1024, 4096], P('seq'), may hold values from -0.1875 to 0.1875
- contract_weight: bfloat16 [4096, 1024], P('seq'), may hold values from -0.09375 to 0.09375
- expand_bias: bfloat16 [4096], P('seq'), may hold values from -3 to 3
- contract_bias: bfloat16 [1024], P('seq'), may hold values from -3 to 3
- norm_gain: bfloat16 [3, 1024], P(None, 'seq'), may hold values from 0.5 to 1.5
- norm_shift: bfloat16 [3, 1024], P(None, 'seq'), may hold values from -3 to 3
Outputs:
- outputs: bfloat16 [8, 13, 256, 1024], P('seq', None, 'tile')
- input_grad: bfloat16 [8, 13, 256, 1024], P('seq', None, 'tile')
- action_table_grad: float32 [8, 1024], P(None, 'seq')
- spatial_inward_grad: float32 [1024, 3072], P('seq')
- spatial_outward_grad: float32 [1024, 1024], P('seq')
- temporal_inward_grad: float32 [1024, 3072], P('seq')
- temporal_outward_grad: float32 [1024, 1024], P('seq')
- expand_weight_grad: float32 [1024, 4096], P('seq')
- contract_weight_grad: float32 [4096, 1024], P('seq')
- expand_bias_grad: float32 [4096], P('seq')
- contract_bias_grad: float32 [1024], P('seq')
- norm_gain_grad: float32 [3, 1024], P(None, 'seq')
- norm_shift_grad: float32 [3, 1024], P(None, 'seq')
Inputs may be any that keep to these rules, and one draw needn't show every extreme that they name: Within a packed sequence the segment ids never fall from frame to frame; each sequence holds 4 segments of at most 6 frames each.
All inputs are finite; a program needn't handle non-finite values.
Results may differ from a plain program's by a relative error of at most 0.018.
Values may be sent and summed in bfloat16 or wider, within the bound.
No kernel may reach another device: no remote copies, remote signals or barrier semaphores. Data moves between devices by JAX's collectives and lax.ppermute only.
A program may use at most 320 MiB of HBM per device.

v0:
```python
import jax
import jax.numpy as jnp
from jax import lax
from jax.sharding import PartitionSpec as P

HEAD = 64
epsilon = 1e-05
masked_score = -1e30


def gelu_tanh(hidden):
    return jax.nn.gelu(hidden, approximate=True)


def norm_parts(hidden, gain_row, shift_row):
    centre = jnp.mean(hidden, axis=-1, keepdims=True)
    centred = hidden - centre
    spread = jnp.mean(centred * centred, axis=-1, keepdims=True)
    inverse = lax.rsqrt(spread + epsilon)
    normed = centred * inverse
    return ((normed * gain_row + shift_row).astype(jnp.bfloat16), normed, inverse)


def norm_back(upstream, normed, inverse, gain_row):
    scaled = upstream * gain_row
    mean_first = jnp.mean(scaled, axis=-1, keepdims=True)
    mean_second = jnp.mean(scaled * normed, axis=-1, keepdims=True)
    grad_back = inverse * (scaled - mean_first - normed * mean_second)
    return (grad_back, jnp.sum(upstream * normed, axis=0), jnp.sum(upstream, axis=0))


def soft_rows(scores):
    row_top = jnp.max(scores, axis=-1, keepdims=True)
    powered = jnp.exp(scores - row_top)
    row_total = jnp.sum(powered, axis=-1, keepdims=True)
    return (powered / row_total, row_top + jnp.log(row_total))


def score_grads(softmaxed, grad_soft):
    inner_sum = jnp.sum(grad_soft * softmaxed, axis=-1, keepdims=True)
    return (softmaxed * (grad_soft - inner_sum)).astype(jnp.bfloat16)


def body(
    inputs,
    actions,
    segments,
    cotangent,
    action_table,
    spatial_inward,
    spatial_outward,
    temporal_inward,
    temporal_outward,
    expand_weight,
    contract_weight,
    expand_bias,
    contract_bias,
    norm_gain,
    norm_shift,
):
    (
        table_full,
        space_in,
        space_out,
        time_in,
        time_out,
        expand_full,
        contract_full,
        expand_shift,
        contract_shift,
        gain_full,
        shift_full,
    ) = (
        lax.all_gather(action_table, "seq", axis=1, tiled=True),
        lax.all_gather(spatial_inward, "seq", axis=0, tiled=True),
        lax.all_gather(spatial_outward, "seq", axis=0, tiled=True),
        lax.all_gather(temporal_inward, "seq", axis=0, tiled=True),
        lax.all_gather(temporal_outward, "seq", axis=0, tiled=True),
        lax.all_gather(expand_weight, "seq", axis=0, tiled=True),
        lax.all_gather(contract_weight, "seq", axis=0, tiled=True),
        lax.all_gather(expand_bias, "seq", axis=0, tiled=True),
        lax.all_gather(contract_bias, "seq", axis=0, tiled=True),
        lax.all_gather(norm_gain, "seq", axis=1, tiled=True),
        lax.all_gather(norm_shift, "seq", axis=1, tiled=True),
    )
    packed_count, frames, tile_cells, model_width = inputs.shape
    row_count = packed_count * frames * tile_cells
    head_count = model_width // HEAD
    score_scale = HEAD ** (-0.5)
    frame_width = tile_cells * lax.axis_size("tile")
    gain_rows = gain_full.astype(jnp.float32)
    shift_rows = shift_full.astype(jnp.float32)
    f32 = jnp.float32
    bf16 = jnp.bfloat16
    onehot = (
        actions[:, :, None] == jnp.arange(table_full.shape[0], dtype=jnp.int32)[None, None, :]
    ).astype(bf16)
    embedded = jnp.einsum("sfa,ad->sfd", onehot, table_full, preferred_element_type=f32)
    embed_sum = (inputs.astype(f32) + embedded[:, :, None, :]).reshape(row_count, model_width)
    normed_one, unit_one, inverse_one = norm_parts(embed_sum, gain_rows[0], shift_rows[0])
    projected = jnp.dot(normed_one, space_in, preferred_element_type=f32).astype(bf16)
    space_query = projected[:, :model_width].reshape(
        packed_count, frames, tile_cells, head_count, HEAD
    )
    own_keys = projected[:, model_width : 2 * model_width].reshape(
        packed_count, frames, tile_cells, model_width
    )
    own_values = projected[:, 2 * model_width :].reshape(
        packed_count, frames, tile_cells, model_width
    )
    frame_keys, frame_values = (
        lax.all_gather(own_keys, "tile", axis=2, tiled=True),
        lax.all_gather(own_values, "tile", axis=2, tiled=True),
    )
    key_heads = frame_keys.reshape(packed_count, frames, frame_width, head_count, HEAD)
    value_heads = frame_values.reshape(packed_count, frames, frame_width, head_count, HEAD)

    def space_scores():
        return (
            jnp.einsum("sfqhd,sfkhd->sfhqk", space_query, key_heads, preferred_element_type=f32)
            * score_scale
        )

    space_soft, space_lse = soft_rows(space_scores())
    space_mixed = jnp.einsum(
        "sfhqk,sfkhd->sfqhd", space_soft.astype(bf16), value_heads, preferred_element_type=f32
    )
    space_mixed = space_mixed.astype(bf16).reshape(row_count, model_width)
    space_sum = embed_sum + jnp.dot(space_mixed, space_out, preferred_element_type=f32)
    normed_two, unit_two, inverse_two = norm_parts(space_sum, gain_rows[1], shift_rows[1])
    time_proj = jnp.dot(normed_two, time_in, preferred_element_type=f32).astype(bf16)
    time_proj = time_proj.reshape(packed_count, frames, tile_cells, 3, head_count, HEAD)
    time_query = time_proj[:, :, :, 0]
    time_keys = time_proj[:, :, :, 1]
    time_values = time_proj[:, :, :, 2]
    frame_index = jnp.arange(frames, dtype=jnp.int32)
    allowed = (frame_index[None, None, :] <= frame_index[None, :, None]) & (
        segments[:, None, :] == segments[:, :, None]
    )
    allowed_heads = allowed[:, None, None, :, :]

    def time_scores():
        raw_scores = (
            jnp.einsum("sfphd,sgphd->sphfg", time_query, time_keys, preferred_element_type=f32)
            * score_scale
        )
        return jnp.where(allowed_heads, raw_scores, masked_score)

    time_soft, time_lse = soft_rows(time_scores())
    time_mixed = jnp.einsum(
        "sphfg,sgphd->sfphd", time_soft.astype(bf16), time_values, preferred_element_type=f32
    )
    time_mixed = time_mixed.astype(bf16).reshape(row_count, model_width)
    time_sum = space_sum + jnp.dot(time_mixed, time_out, preferred_element_type=f32)
    normed_three, unit_three, inverse_three = norm_parts(time_sum, gain_rows[2], shift_rows[2])
    expanded = jnp.dot(normed_three, expand_full, preferred_element_type=f32) + expand_shift.astype(
        f32
    )
    activated, gelu_pull = jax.vjp(gelu_tanh, expanded)
    activated_low = activated.astype(bf16)
    block_out = (
        time_sum
        + jnp.dot(activated_low, contract_full, preferred_element_type=f32)
        + contract_shift.astype(f32)
    )
    outputs = block_out.astype(bf16).reshape(inputs.shape)
    upstream = cotangent.astype(f32).reshape(row_count, model_width)
    grad_contract_shift = jnp.sum(upstream, axis=0)
    upstream_low = upstream.astype(bf16)
    grad_contract = jnp.einsum("rf,rd->fd", activated_low, upstream_low, preferred_element_type=f32)
    grad_activated = jnp.einsum(
        "rd,fd->rf", upstream_low, contract_full, preferred_element_type=f32
    )
    grad_expanded = gelu_pull(grad_activated)[0].astype(bf16)
    grad_expand_shift = jnp.sum(grad_expanded.astype(f32), axis=0)
    grad_expand = jnp.einsum("rd,rf->df", normed_three, grad_expanded, preferred_element_type=f32)
    grad_normed_three = jnp.einsum(
        "rf,df->rd", grad_expanded, expand_full, preferred_element_type=f32
    )
    back_three, gain_three, shift_three = norm_back(
        grad_normed_three, unit_three, inverse_three, gain_rows[2]
    )
    grad_time_sum = upstream + back_three
    time_low = grad_time_sum.astype(bf16)
    grad_time_out = jnp.einsum("rd,re->de", time_mixed, time_low, preferred_element_type=f32)
    grad_time_mixed = jnp.einsum(
        "re,de->rd", time_low, time_out, preferred_element_type=f32
    ).astype(bf16)
    grad_time_mixed = grad_time_mixed.reshape(packed_count, frames, tile_cells, head_count, HEAD)
    time_again = jnp.exp(time_scores() - time_lse)
    grad_time_values = jnp.einsum(
        "sphfg,sfphd->sgphd", time_again.astype(bf16), grad_time_mixed, preferred_element_type=f32
    )
    grad_time_soft = jnp.einsum(
        "sfphd,sgphd->sphfg", grad_time_mixed, time_values, preferred_element_type=f32
    )
    grad_time_scores = score_grads(time_again, grad_time_soft)
    grad_time_query = (
        jnp.einsum("sphfg,sgphd->sfphd", grad_time_scores, time_keys, preferred_element_type=f32)
        * score_scale
    )
    grad_time_keys = (
        jnp.einsum("sphfg,sfphd->sgphd", grad_time_scores, time_query, preferred_element_type=f32)
        * score_scale
    )
    grad_time_proj = jnp.stack([grad_time_query, grad_time_keys, grad_time_values], axis=3).astype(
        bf16
    )
    grad_time_proj = grad_time_proj.reshape(row_count, 3 * model_width)
    grad_time_in = jnp.einsum("rd,re->de", normed_two, grad_time_proj, preferred_element_type=f32)
    grad_normed_two = jnp.einsum("re,de->rd", grad_time_proj, time_in, preferred_element_type=f32)
    back_two, gain_two, shift_two = norm_back(grad_normed_two, unit_two, inverse_two, gain_rows[1])
    grad_space_sum = grad_time_sum + back_two
    space_low = grad_space_sum.astype(bf16)
    grad_space_out = jnp.einsum("rd,re->de", space_mixed, space_low, preferred_element_type=f32)
    grad_space_mixed = jnp.einsum(
        "re,de->rd", space_low, space_out, preferred_element_type=f32
    ).astype(bf16)
    grad_space_mixed = grad_space_mixed.reshape(packed_count, frames, tile_cells, head_count, HEAD)
    space_again = jnp.exp(space_scores() - space_lse)
    grad_space_soft = jnp.einsum(
        "sfqhd,sfkhd->sfhqk", grad_space_mixed, value_heads, preferred_element_type=f32
    )
    grad_space_scores = score_grads(space_again, grad_space_soft)
    grad_space_query = (
        jnp.einsum("sfhqk,sfkhd->sfqhd", grad_space_scores, key_heads, preferred_element_type=f32)
        * score_scale
    )
    grad_frame_values = jnp.einsum(
        "sfhqk,sfqhd->sfkhd", space_again.astype(bf16), grad_space_mixed, preferred_element_type=f32
    )
    grad_frame_keys = (
        jnp.einsum("sfhqk,sfqhd->sfkhd", grad_space_scores, space_query, preferred_element_type=f32)
        * score_scale
    )
    grad_frame_keys = grad_frame_keys.reshape(packed_count, frames, frame_width, model_width)
    grad_frame_values = grad_frame_values.reshape(packed_count, frames, frame_width, model_width)
    own_grad_keys, own_grad_values = (
        lax.psum_scatter(
            grad_frame_keys.astype(jnp.bfloat16), "tile", scatter_dimension=2, tiled=True
        ).astype(jnp.float32),
        lax.psum_scatter(
            grad_frame_values.astype(jnp.bfloat16), "tile", scatter_dimension=2, tiled=True
        ).astype(jnp.float32),
    )
    grad_space_proj = jnp.concatenate(
        [
            grad_space_query.reshape(row_count, model_width),
            own_grad_keys.reshape(row_count, model_width),
            own_grad_values.reshape(row_count, model_width),
        ],
        axis=1,
    ).astype(bf16)
    grad_space_in = jnp.einsum("rd,re->de", normed_one, grad_space_proj, preferred_element_type=f32)
    grad_normed_one = jnp.einsum("re,de->rd", grad_space_proj, space_in, preferred_element_type=f32)
    back_one, gain_one, shift_one = norm_back(grad_normed_one, unit_one, inverse_one, gain_rows[0])
    grad_embed_sum = grad_space_sum + back_one
    input_grad = grad_embed_sum.astype(bf16).reshape(inputs.shape)
    per_frame = jnp.sum(
        grad_embed_sum.reshape(packed_count, frames, tile_cells, model_width), axis=2
    )
    grad_table = jnp.einsum(
        "sfa,sfd->ad", onehot.astype(f32), per_frame, precision=lax.Precision.HIGHEST
    )
    grad_gains = jnp.stack([gain_one, gain_two, gain_three], axis=0)
    grad_shifts = jnp.stack([shift_one, shift_two, shift_three], axis=0)
    local_grads = (
        grad_table,
        grad_space_in,
        grad_space_out,
        grad_time_in,
        grad_time_out,
        grad_expand,
        grad_contract,
        grad_expand_shift,
        grad_contract_shift,
        grad_gains,
        grad_shifts,
    )
    shards = (
        lax.psum_scatter(
            local_grads[0].astype(jnp.bfloat16), "seq", scatter_dimension=1, tiled=True
        ).astype(jnp.float32),
        lax.psum_scatter(
            local_grads[1].astype(jnp.bfloat16), "seq", scatter_dimension=0, tiled=True
        ).astype(jnp.float32),
        lax.psum_scatter(
            local_grads[2].astype(jnp.bfloat16), "seq", scatter_dimension=0, tiled=True
        ).astype(jnp.float32),
        lax.psum_scatter(
            local_grads[3].astype(jnp.bfloat16), "seq", scatter_dimension=0, tiled=True
        ).astype(jnp.float32),
        lax.psum_scatter(
            local_grads[4].astype(jnp.bfloat16), "seq", scatter_dimension=0, tiled=True
        ).astype(jnp.float32),
        lax.psum_scatter(
            local_grads[5].astype(jnp.bfloat16), "seq", scatter_dimension=0, tiled=True
        ).astype(jnp.float32),
        lax.psum_scatter(
            local_grads[6].astype(jnp.bfloat16), "seq", scatter_dimension=0, tiled=True
        ).astype(jnp.float32),
        lax.psum_scatter(
            local_grads[7].astype(jnp.bfloat16), "seq", scatter_dimension=0, tiled=True
        ).astype(jnp.float32),
        lax.psum_scatter(
            local_grads[8].astype(jnp.bfloat16), "seq", scatter_dimension=0, tiled=True
        ).astype(jnp.float32),
        lax.psum_scatter(
            local_grads[9].astype(jnp.bfloat16), "seq", scatter_dimension=1, tiled=True
        ).astype(jnp.float32),
        lax.psum_scatter(
            local_grads[10].astype(jnp.bfloat16), "seq", scatter_dimension=1, tiled=True
        ).astype(jnp.float32),
    )
    summed = (
        lax.psum(shards[0].astype(jnp.bfloat16), "tile").astype(jnp.float32),
        lax.psum(shards[1].astype(jnp.bfloat16), "tile").astype(jnp.float32),
        lax.psum(shards[2].astype(jnp.bfloat16), "tile").astype(jnp.float32),
        lax.psum(shards[3].astype(jnp.bfloat16), "tile").astype(jnp.float32),
        lax.psum(shards[4].astype(jnp.bfloat16), "tile").astype(jnp.float32),
        lax.psum(shards[5].astype(jnp.bfloat16), "tile").astype(jnp.float32),
        lax.psum(shards[6].astype(jnp.bfloat16), "tile").astype(jnp.float32),
        lax.psum(shards[7].astype(jnp.bfloat16), "tile").astype(jnp.float32),
        lax.psum(shards[8].astype(jnp.bfloat16), "tile").astype(jnp.float32),
        lax.psum(shards[9].astype(jnp.bfloat16), "tile").astype(jnp.float32),
        lax.psum(shards[10].astype(jnp.bfloat16), "tile").astype(jnp.float32),
    )
    return (
        outputs,
        input_grad,
        summed[0],
        summed[1],
        summed[2],
        summed[3],
        summed[4],
        summed[5],
        summed[6],
        summed[7],
        summed[8],
        summed[9],
        summed[10],
    )


def solution(mesh):
    placed = (
        P("seq", None, "tile", None),
        P("seq", None),
        P("seq", None),
        P("seq", None, "tile", None),
        P(None, "seq"),
        P("seq", None),
        P("seq", None),
        P("seq", None),
        P("seq", None),
        P("seq", None),
        P("seq", None),
        P("seq"),
        P("seq"),
        P(None, "seq"),
        P(None, "seq"),
    )
    return jax.shard_map(
        body,
        mesh=mesh,
        in_specs=placed,
        out_specs=(
            P("seq", None, "tile", None),
            P("seq", None, "tile", None),
            P(None, "seq"),
            P("seq", None),
            P("seq", None),
            P("seq", None),
            P("seq", None),
            P("seq", None),
            P("seq", None),
            P("seq"),
            P("seq"),
            P(None, "seq"),
            P(None, "seq"),
        ),
        check_vma=False,
    )
```

profile of v0, /device:TPU:0, one launch (start us, length us, event | category | flops | bytes accessed | tf_op | source)
XLA Modules:
  0.0 1583.9 jit_solution(6852255820230631596)
XLA Ops:
  8.0 10.5 all_gather.39
  23.7 8.9 all_gather.40
  42.3 15.9 %all-gather.11.cloned.1.call-done = bf16[1024,3072]{1,0:T(8,128)(2,1)} async-done(((bf16[128,3072]{1,0:T(8,128)(2,1)}), bf16[1024,3072]{1,0:T(8,128)(2,1)}) %all-gather.11.cloned.1.call-update) | async-done | bytes 6291472 | tf_op jit(solution)/shard_map/all_gather | solution.py:75
  58.2 8.0 convolution_convert_fusion.6
  72.9 9.0 all-gather
  91.1 101.7 %all-gather.15.cloned.1.call-done = bf16[1,13,256,1024]{3,2,1,0:T(8,128)(2,1)} async-done(((bf16[1,13,64,1024]{3,2,1,0:T(8,128)(2,1)}), bf16[1,13,256,1024]{3,2,1,0:T(8,128)(2,1)}) %all-gather.15.cloned.1.call-update) | async-done | bytes 6815760 | tf_op jit(solution)/shard_map/all_gather | solution.py:112
  192.8 10.3 copy.61
  203.2 114.0 %all-gather.13.cloned.1.call-done = bf16[1,13,256,1024]{3,2,1,0:T(8,128)(2,1)} async-done(((bf16[1,13,64,1024]{3,2,1,0:T(8,128)(2,1)}), bf16[1,13,256,1024]{3,2,1,0:T(8,128)(2,1)}) %all-gather.13.cloned.1.call-update) | async-done | bytes 6815760 | tf_op jit(solution)/shard_map/all_gather | solution.py:113
  317.1 10.3 copy.60
  339.3 8.1 convert_bitcast_fusion.2
  365.9 26.4 %all-gather.19.cloned.1.call-done = bf16[1024,3072]{1,0:T(8,128)(2,1)} async-done(((bf16[128,3072]{1,0:T(8,128)(2,1)}), bf16[1024,3072]{1,0:T(8,128)(2,1)}) %all-gather.19.cloned.1.call-update) | async-done | bytes 6291472 | tf_op jit(solution)/shard_map/all_gather | solution.py:77
  392.3 10.5 convolution_convert_fusion.5
  402.8 13.3 reshape.501
  450.2 28.1 %all-gather.23.cloned.1.call-done = bf16[1024,4096]{1,0:T(8,128)(2,1)} async-done(((bf16[128,4096]{1,0:T(8,128)(2,1)}), bf16[1024,4096]{1,0:T(8,128)(2,1)}) %all-gather.23.cloned.1.call-update) | async-done | bytes 8388624 | tf_op jit(solution)/shard_map/all_gather | solution.py:79
  478.3 13.9 fusion.51
  492.1 42.4 %all-gather.25.cloned.1.call-done = bf16[4096,1024]{1,0:T(8,128)(2,1)} async-done(((bf16[512,1024]{1,0:T(8,128)(2,1)}), bf16[4096,1024]{1,0:T(8,128)(2,1)}) %all-gather.25.cloned.1.call-update) | async-done | bytes 8388624 | tf_op jit(solution)/shard_map/all_gather | solution.py:80
  534.6 22.3 %fusion.52 = (bf16[4096]{0:T(1024)(128)(2,1)}, bf16[832,4096]{1,0:T(8,128)(2,1)}) fusion(f32[832,4096]{1,0:T(8,128)} %fusion.51, f32[4096]{0:T(1024)S(1)} %bitcast.176, bf16[832,1024]{1,0:T(8,128)(2,1)} %bitcast.155, bf16[4096,1024]{1,0:T(8,128)(2,1)} %all-gather.25.cloned.1.call-done), kind=kOutput, calls=%fused_computation.128 | convolution fusion | flops 7054290944 | bytes 30564352 | tf_op jit(solution)/shard_map/rd,fd->rf/dot_general | solution.py:171
  556.9 13.3 multiply_reduce_fusion.3
  581.1 8.9 convert_bitcast_fusion
  590.0 12.0 multiply_reduce_fusion.2
  602.0 8.1 multiply_convert_fusion.5
  625.6 13.8 convert_element_type.256
  639.5 10.2 multiply_reduce_fusion.4
  663.9 8.1 convolution_convert_fusion.2
  672.0 10.3 copy.78
  682.3 13.3 multiply_reduce_fusion
  695.6 10.4 multiply_convert_fusion.1
  711.1 10.2 copy.76
  733.3 12.1 convolution_convert_fusion.3
  746.9 16.9 %convolution_convert_fusion = bf16[4096,1024]{1,0:T(8,128)(2,1)} fusion(bf16[832,1024]{1,0:T(8,128)(2,1)S(1)} %bitcast.156, f32[832,4096]{1,0:T(8,128)} %fusion.51, f32[4096]{0:T(1024)S(1)} %bitcast.177), kind=kOutput, calls=%fused_computation.28 | convolution fusion | flops 7017594880 | bytes 23740416 | tf_op jit(solution)/shard_map/rf,rd->fd/dot_general | solution.py:170
  765.8 14.6 convolution_convert_fusion.1
  780.4 8.7 fusion.28
  801.7 121.9 %reduce-scatter.18.cloned.1.call-done = bf16[1,13,64,1024]{3,2,1,0:T(8,128)(2,1)} async-done(((bf16[1,13,256,1024]{3,2,1,0:T(8,128)(2,1)}), bf16[1,13,64,1024]{3,2,1,0:T(8,128)(2,1)}) %reduce-scatter.18.cloned.1.call-update) | async-done | bytes 1703952 | tf_op jit(solution)/shard_map/reduce_scatter | solution.py:239
  923.6 11.4 convolution_convert_fusion.4
  937.2 12.5 multiply_reduce_fusion.5
  960.5 8.8 reduce-scatter.28.cloned.1.call-done
  969.2 45.3 %reduce-scatter.24.cloned.1.call-done = bf16[128,1024]{1,0:T(8,128)(2,1)} async-done(((bf16[1024,1024]{1,0:T(8,128)(2,1)}), bf16[128,1024]{1,0:T(8,128)(2,1)}) %reduce-scatter.24.cloned.1.call-update) | async-done | bytes 262160 | tf_op jit(solution)/shard_map/reduce_scatter | solution.py:287
  1014.6 65.2 %reduce-scatter.26.cloned.1.call-done = bf16[128,3072]{1,0:T(8,128)(2,1)} async-done(((bf16[1024,3072]{1,0:T(8,128)(2,1)}), bf16[128,3072]{1,0:T(8,128)(2,1)}) %reduce-scatter.26.cloned.1.call-update) | async-done | bytes 786448 | tf_op jit(solution)/shard_map/reduce_scatter | solution.py:290
  1079.8 75.0 %reduce-scatter.32.cloned.1.call-done = bf16[512,1024]{1,0:T(8,128)(2,1)} async-done(((bf16[4096,1024]{1,0:T(8,128)(2,1)}), bf16[512,1024]{1,0:T(8,128)(2,1)}) %reduce-scatter.32.cloned.1.call-update) | async-done | bytes 1048592 | tf_op jit(solution)/shard_map/reduce_scatter | solution.py:299
  1154.8 74.6 %reduce-scatter.30.cloned.1.call-done = bf16[128,4096]{1,0:T(8,128)(2,1)} async-done(((bf16[1024,4096]{1,0:T(8,128)(2,1)}), bf16[128,4096]{1,0:T(8,128)(2,1)}) %reduce-scatter.30.cloned.1.call-update) | async-done | bytes 1048592 | tf_op jit(solution)/shard_map/reduce_scatter | solution.py:296
  1229.4 65.4 %reduce-scatter.22.cloned.1.call-done = bf16[128,3072]{1,0:T(8,128)(2,1)} async-done(((bf16[1024,3072]{1,0:T(8,128)(2,1)}), bf16[128,3072]{1,0:T(8,128)(2,1)}) %reduce-scatter.22.cloned.1.call-update) | async-done | bytes 786448 | tf_op jit(solution)/shard_map/reduce_scatter | solution.py:284
  1298.4 8.6 all-gather.1
  1307.1 23.7 %all-reduce.2 = (bf16[4096]{0:T(1024)(128)(2,1)S(1)}, bf16[1024]{0:T(1024)(128)(2,1)S(1)}) all-reduce(bf16[4096]{0:T(1024)(128)(2,1)S(1)} %copy-done.54, bf16[1024]{0:T(1024)(128)(2,1)S(1)} %reduce_sum.249), channel_id=11, replica_groups=mesh['seq'=8,'tile'=4] {'seq'}, use_global_device_ids=true, to_apply=%region_36.37.clone | all-reduce | flops 5120 | bytes 20480
  1330.9 15.2 add_convert_fusion
  1346.9 22.3 %reduce-scatter.36.cloned.1.call-done = bf16[128,3]{1,0:T(8,128)(2,1)} async-done(((bf16[1024,3]{1,0:T(8,128)(2,1)}), bf16[128,3]{1,0:T(8,128)(2,1)}) %reduce-scatter.36.cloned.1.call-update) | async-done | bytes 784
  1370.0 36.5 %reduce-scatter.34.cloned.1.call-done = bf16[128,8]{1,0:T(8,128)(2,1)} async-done(((bf16[1024,8]{1,0:T(8,128)(2,1)}), bf16[128,8]{1,0:T(8,128)(2,1)}) %reduce-scatter.34.cloned.1.call-update) | async-done | bytes 2064
  1407.3 12.0 all-reduce.3
  1422.1 144.1 %all-reduce.7.cloned.1.call-done = (bf16[128,3072]{1,0:T(8,128)(2,1)}, bf16[128,1024]{1,0:T(8,128)(2,1)}, bf16[128,3072]{1,0:T(8,128)(2,1)}, bf16[128,1024]{1,0:...) async-done(((bf16[128,3072]{1,0:T(8,128)(2,1)}, bf16[128,1024]{1,0:T(8,128)(2,1)}, bf16[128,3072]{1,0:T(8,128)(2,1)}, bf16[128,1024]{1,0:T(8,128)(2,1)}, ...) | async-done | bytes 4194320 | tf_op jit(solution)/shard_map/psum | solution.py:317
  (275 shorter events, 200.4 us)
Async XLA Ops:
  7.2 16.5 %copy-start.63 = (bf16[3,128]{1,0:T(4,128)(2,1)S(1)}, bf16[3,128]{1,0:T(4,128)(2,1)}, u32[]{:S(2)}) copy-start(bf16[3,128]{1,0:T(4,128)(2,1)} %param.28) | copy-start | bytes 2308
  7.2 25.4 %copy-start.64 = (bf16[3,128]{1,0:T(4,128)(2,1)S(1)}, bf16[3,128]{1,0:T(4,128)(2,1)}, u32[]{:S(2)}) copy-start(bf16[3,128]{1,0:T(4,128)(2,1)} %param.29) | copy-start | bytes 2308
  7.2 51.0 %all-gather.11.cloned.1.call-start = ((), (), s32[]{:S(2)}) async-start(), calls=%async_computation.11 | async-start | bytes 7077888 | tf_op jit(solution)/shard_map/all_gather | solution.py:75
  7.9 184.9 %all-gather.15.cloned.1.call-start = ((), (), s32[]{:S(2)}) async-start(), calls=%async_computation.13 | async-start | bytes 8519680 | tf_op jit(solution)/shard_map/all_gather | solution.py:112
  21.5 20.9 %copy-start.36 = (f32[832]{0:T(1024)}, f32[832]{0:T(1024)S(1)}, u32[]{:S(2)}) copy-start(f32[832]{0:T(1024)S(1)} %div.57) | copy-start | bytes 9988
  23.6 42.7 %copy-start.4 = (f32[1,13,64,1024]{3,2,1,0:T(8,128)}, f32[1,13,64,1024]{3,2,1,0:T(8,128)S(1)}, u32[]{:S(2)}) copy-start(f32[1,13,64,1024]{3,2,1,0:T(8,128)S(1)} %get-tuple-element.49) | copy-start | bytes 10223620
  23.7 42.6 %copy-start.38 = (f32[832]{0:T(1024)}, f32[832]{0:T(1024)S(1)}, u32[]{:S(2)}) copy-start(f32[832]{0:T(1024)S(1)} %rsqrt.28) | copy-start | bytes 9988
  40.5 25.8 %copy-start.42 = (f32[1,1024]{1,0:T(1,128)}, f32[1,1024]{1,0:T(1,128)S(1)}, u32[]{:S(2)}) copy-start(f32[1,1024]{1,0:T(1,128)S(1)} %get-tuple-element.52) | copy-start | bytes 12292
  40.5 351.8 %copy-start.46 = (f32[1,1024]{1,0:T(1,128)}, f32[1,1024]{1,0:T(1,128)S(1)}, u32[]{:S(2)}) copy-start(f32[1,1024]{1,0:T(1,128)S(1)} %get-tuple-element.51) | copy-start | bytes 12292
  40.5 529.7 %copy-start.50 = (f32[1,1024]{1,0:T(1,128)}, f32[1,1024]{1,0:T(1,128)S(1)}, u32[]{:S(2)}) copy-start(f32[1,1024]{1,0:T(1,128)S(1)} %get-tuple-element.50) | copy-start | bytes 12292
  40.5 351.8 %copy-start.57 = (f32[1,1024]{1,0:T(1,128)}, f32[1,1024]{1,0:T(1,128)S(1)}, u32[]{:S(2)}) copy-start(f32[1,1024]{1,0:T(1,128)S(1)} %get-tuple-element.54) | copy-start | bytes 12292
  40.5 437.7 %copy-start.55 = (f32[1,1024]{1,0:T(1,128)}, f32[1,1024]{1,0:T(1,128)S(1)}, u32[]{:S(2)}) copy-start(f32[1,1024]{1,0:T(1,128)S(1)} %get-tuple-element.53) | copy-start | bytes 12292
  68.8 248.4 %all-gather.13.cloned.1.call-start = ((), (), s32[]{:S(2)}) async-start(), calls=%async_computation.12 | async-start | bytes 8519680 | tf_op jit(solution)/shard_map/all_gather | solution.py:113
  69.5 290.1 %all-gather.17.cloned.1.call-start = ((), (), s32[]{:S(2)}) async-start(), calls=%async_computation.14 | async-start | bytes 2359296 | tf_op jit(solution)/shard_map/all_gather | solution.py:76
  70.1 322.2 %all-gather.19.cloned.1.call-start = ((), (), s32[]{:S(2)}) async-start(), calls=%async_computation.15 | async-start | bytes 7077888 | tf_op jit(solution)/shard_map/all_gather | solution.py:77
  70.7 371.8 %all-gather.21.cloned.1.call-start = ((), (), s32[]{:S(2)}) async-start(), calls=%async_computation.16 | async-start | bytes 2359296 | tf_op jit(solution)/shard_map/all_gather | solution.py:78
  71.2 407.0 %all-gather.23.cloned.1.call-start = ((), (), s32[]{:S(2)}) async-start(), calls=%async_computation.17 | async-start | bytes 9437184 | tf_op jit(solution)/shard_map/all_gather | solution.py:79
  72.0 462.6 %all-gather.25.cloned.1.call-start = ((), (), s32[]{:S(2)}) async-start(), calls=%async_computation.18 | async-start | bytes 9437184 | tf_op jit(solution)/shard_map/all_gather | solution.py:80
  72.7 729.0 %reduce-scatter.20.cloned.1.call-start = ((), (), s32[]{:S(2)}) async-start(), calls=%async_computation.20 | async-start | bytes 8519680 | tf_op jit(solution)/shard_map/reduce_scatter | solution.py:242
  81.9 452.6 %copy-start.52 = (f32[8,1,512]{2,1,0:T(1,128)}, f32[8,1,512]{2,1,0:T(1,128)S(1)}, u32[]{:S(2)}) copy-start(f32[8,1,512]{2,1,0:T(1,128)S(1)} %convert_element_type.288) | copy-start | bytes 49156
  338.4 9.0 copy-start.32
  363.7 39.1 %copy-start.34 = (f32[832]{0:T(1024)}, f32[832]{0:T(1024)S(1)}, u32[]{:S(2)}) copy-start(f32[832]{0:T(1024)S(1)} %broadcast_multiply_fusion.8) | copy-start | bytes 9988
  365.9 36.9 %copy-start.44 = (f32[832]{0:T(1024)}, f32[832]{0:T(1024)S(1)}, u32[]{:S(2)}) copy-start(f32[832]{0:T(1024)S(1)} %add_rsqrt_fusion.2) | copy-start | bytes 9988
  447.7 122.6 %copy-start.15 = (f32[832,1024]{1,0:T(8,128)}, f32[832,1024]{1,0:T(8,128)S(1)}, u32[]{:S(2)}) copy-start(f32[832,1024]{1,0:T(8,128)S(1)} %get-tuple-element.63) | copy-start | bytes 10223620
  447.7 122.6 %copy-start.40 = (f32[832]{0:T(1024)}, f32[832]{0:T(1024)S(1)}, u32[]{:S(2)}) copy-start(f32[832]{0:T(1024)S(1)} %broadcast_multiply_fusion.7) | copy-start | bytes 9988
  448.2 122.1 %copy-start.48 = (f32[832]{0:T(1024)}, f32[832]{0:T(1024)S(1)}, u32[]{:S(2)}) copy-start(f32[832]{0:T(1024)S(1)} %add_rsqrt_fusion.1) | copy-start | bytes 9988
  556.9 13.4 copy-start.22
  625.6 13.9 copy-start.19
  625.6 13.9 copy-start.35
  625.6 13.9 copy-start.45
  625.6 13.9 copy-start.47
  639.5 10.3 copy-start.21
  682.3 241.3 %reduce-scatter.18.cloned.1.call-start = ((), (), s32[]{:S(2)}) async-start(), calls=%async_computation.19 | async-start | bytes 8519680 | tf_op jit(solution)/shard_map/reduce_scatter | solution.py:239
  695.6 10.4 copy-start.3
  721.4 247.8 %reduce-scatter.28.cloned.1.call-start = ((), (), s32[]{:S(2)}) async-start(), calls=%async_computation.24 | async-start | bytes 2359296 | tf_op jit(solution)/shard_map/reduce_scatter | solution.py:293
  727.8 286.8 %reduce-scatter.24.cloned.1.call-start = ((), (), s32[]{:S(2)}) async-start(), calls=%async_computation.22 | async-start | bytes 2359296 | tf_op jit(solution)/shard_map/reduce_scatter | solution.py:287
  733.3 346.5 %reduce-scatter.26.cloned.1.call-start = ((), (), s32[]{:S(2)}) async-start(), calls=%async_computation.23 | async-start | bytes 7077888 | tf_op jit(solution)/shard_map/reduce_scatter | solution.py:290
  745.5 409.3 %reduce-scatter.32.cloned.1.call-start = ((), (), s32[]{:S(2)}) async-start(), calls=%async_computation.26 | async-start | bytes 9437184 | tf_op jit(solution)/shard_map/reduce_scatter | solution.py:299
  763.9 465.5 %reduce-scatter.30.cloned.1.call-start = ((), (), s32[]{:S(2)}) async-start(), calls=%async_computation.25 | async-start | bytes 9437184 | tf_op jit(solution)/shard_map/reduce_scatter | solution.py:296
  780.4 514.3 %reduce-scatter.22.cloned.1.call-start = ((), (), s32[]{:S(2)}) async-start(), calls=%async_computation.21 | async-start | bytes 7077888 | tf_op jit(solution)/shard_map/reduce_scatter | solution.py:284
  935.1 411.0 %reduce-scatter.38.cloned.1.call-start = ((), (), s32[]{:S(2)}) async-start(), calls=%async_computation.29 | async-start | bytes 294912
  950.6 418.6 %reduce-scatter.36.cloned.1.call-start = ((), (), s32[]{:S(2)}) async-start(), calls=%async_computation.28 | async-start | bytes 294912
  956.7 338.1 %copy-start.69 = (u32[32]{0:T(128)S(1)}, u32[32]{0:T(128)}, u32[]{:S(2)}) copy-start(u32[32]{0:T(128)} %constant.48) | copy-start | bytes 388
  959.1 339.3 %copy-start.66 = (bf16[128]{0:T(256)(128)(2,1)S(1)}, bf16[128]{0:T(256)(128)(2,1)}, u32[]{:S(2)}) copy-start(bf16[128]{0:T(256)(128)(2,1)} %param.27) | copy-start | bytes 772
  959.2 347.9 %copy-start.54 = (bf16[4096]{0:T(1024)(128)(2,1)S(1)}, bf16[4096]{0:T(1024)(128)(2,1)}, u32[]{:S(2)}) copy-start(bf16[4096]{0:T(1024)(128)(2,1)} %get-tuple-element.38) | copy-start | bytes 24580
  959.2 371.8 %copy-start.17 = (f32[832,1024]{1,0:T(8,128)S(1)}, f32[832,1024]{1,0:T(8,128)}, u32[]{:S(2)}) copy-start(f32[832,1024]{1,0:T(8,128)} %copy-done.15) | copy-start | bytes 10223620
  959.2 447.3 %reduce-scatter.34.cloned.1.call-start = ((), (), s32[]{:S(2)}) async-start(), calls=%async_computation.27 | async-start | bytes 294912
  960.4 605.8 %all-reduce.7.cloned.1.call-start = ((), (), s32[]{:S(2)}) async-start(), calls=%async_computation.30 | async-start | bytes 8388608 | tf_op jit(solution)/shard_map/psum | solution.py:317
  (42 other events, 166.3 us)
Sparse Core Ops, SparseCore 0:
  9.9 48.2 all-gather.10
  68.9 123.9 all-gather.14
  195.0 122.0 all-gather.12
  318.9 26.0 all-gather.16
  346.7 45.5 all-gather.18
  394.0 27.8 all-gather.20
  423.8 54.3 all-gather.22
  480.1 54.3 all-gather.24
  682.4 119.2 reduce-scatter.19
  803.8 119.7 reduce-scatter.17
  927.5 41.6 reduce-scatter.27
  973.3 41.2 reduce-scatter.23
  1018.0 61.7 reduce-scatter.25
  1083.5 71.2 reduce-scatter.31
  1158.1 71.2 reduce-scatter.29
  1233.0 61.7 reduce-scatter.21
  1298.2 33.6 reduce-scatter.37
  1335.6 33.5 reduce-scatter.35
  1372.8 33.6 reduce-scatter.33
  1409.4 156.7 all-reduce.6
where the time goes:
time: 1590 us; the launch traced here: 1580 us
  waiting for transfers between devices  996 us (63%)
  matrix products  276 us (17%)
  local copies, waits for them, and re-layouts  149 us (9%)
  blocking collectives  80.6 us (5%)
  other arithmetic  64.8 us (4%)
  between operations  16.6 us (1%)
    psum x1, waiting for transfers between devices, body(): lax.psum(shards[1].astype(jnp.bfloat16), 'tile').astype(jnp.float32)  144 us
    reduce_scatter x1, waiting for transfers between devices, body(): lax.psum_scatter(grad_frame_keys.astype(jnp.bfloat16), 'tile', scatter_di...  122 us
    all_gather x1, waiting for transfers between devices, body(): lax.all_gather(own_values, 'tile', axis=2, tiled=True)  114 us
    all_gather x1, waiting for transfers between devices, body(): lax.all_gather(own_keys, 'tile', axis=2, tiled=True)  102 us
    reduce_scatter x1, waiting for transfers between devices, body(): lax.psum_scatter(local_grads[6].astype(jnp.bfloat16), 'seq', scatter_dime...  75 us
    reduce_scatter x1, waiting for transfers between devices, body(): lax.psum_scatter(local_grads[5].astype(jnp.bfloat16), 'seq', scatter_dime...  74.6 us
    reduce_scatter x1, waiting for transfers between devices, body(): lax.psum_scatter(local_grads[1].astype(jnp.bfloat16), 'seq', scatter_dime...  65.4 us
    reduce_scatter x1, waiting for transfers between devices, body(): lax.psum_scatter(local_grads[3].astype(jnp.bfloat16), 'seq', scatter_dime...  65.2 us
  transfers between devices with their start and end apart: 20, of which 17 were waited for; matrix products, arithmetic and copies ran while one was open for 20% of the time, Pallas kernels for 0%

commit v1 on v0

--- a/solution.py
+++ b/solution.py
@@ -58,6 +58,25 @@
     norm_gain,
     norm_shift,
 ):
+
+    def attach_ratios(xin, bus_axis):
+        h_now = jax.lax.axis_size(bus_axis)
+        work_now = jax.lax.axis_index(bus_axis)
+        reached, even, later = (h_now, work_now, xin.shape[0])
+        odd, e_next = (xin, 1)
+        while e_next < reached:
+            odd = jnp.concatenate(
+                [
+                    odd,
+                    jax.lax.ppermute(
+                        odd, bus_axis, [(jj, (jj - e_next) % reached) for jj in range(reached)]
+                    ),
+                ],
+                0,
+            )
+            e_next = 2 * e_next
+        return jnp.roll(odd, even * later, 0)
+
     (
         table_full,
         space_in,
@@ -77,7 +96,7 @@
         lax.all_gather(temporal_inward, "seq", axis=0, tiled=True),
         lax.all_gather(temporal_outward, "seq", axis=0, tiled=True),
         lax.all_gather(expand_weight, "seq", axis=0, tiled=True),
-        lax.all_gather(contract_weight, "seq", axis=0, tiled=True),
+        attach_ratios(contract_weight, "seq"),
         lax.all_gather(expand_bias, "seq", axis=0, tiled=True),
         lax.all_gather(contract_bias, "seq", axis=0, tiled=True),
         lax.all_gather(norm_gain, "seq", axis=1, tiled=True),

time: 1590 us -> 1550 us (0.975)
  waiting for transfers between devices: 996 us -> 842 us
  blocking collectives: 80.6 us -> 167 us
  local copies, waits for them, and re-layouts: 149 us -> 165 us
    all_gather x1, waiting for transfers between devices: 114 us -> 0.01 us  [body(): lax.all_gather(own_values, 'tile', axis=2, tiled=True)]
    all_gather x1, blocking collectives: 9.03 us -> 95.4 us  [body(): lax.all_gather(expand_bias, 'seq', axis=0, tiled=True)]
    ppermute x0 -> x3, waiting for transfers between devices: none -> 58.8 us  [attach_ratios(): jax.lax.ppermute(odd, bus_axis, [(jj, (jj - e_next) % reached) for jj in...]
    all_gather x1, waiting for transfers between devices: 102 us -> 48.4 us  [body(): lax.all_gather(own_keys, 'tile', axis=2, tiled=True)]
    all_gather x1 -> x0, waiting for transfers between devices: 42.4 us -> none  [body(): lax.all_gather(contract_weight, 'seq', axis=0, tiled=True)]
    reduce_scatter x1, waiting for transfers between devices: 8.78 us -> 45.5 us  [body(): lax.psum_scatter(local_grads[4].astype(jnp.bfloat16), 'seq', scatter_dime...]
    reduce_scatter x1, waiting for transfers between devices: 45.3 us -> 8.69 us  [body(): lax.psum_scatter(local_grads[2].astype(jnp.bfloat16), 'seq', scatter_dime...]
    unnamed x23 -> x22, waiting for transfers between devices: 63.3 us -> 60.8 us
  transfers between devices with their start and end apart: 20 -> 22, of which waited for: 17 -> 17; matrix products, arithmetic and copies ran while one was open for 20% -> 20% of each run, Pallas kernels for 0% -> 0%
where the time goes in v1:
time: 1550 us; the launch traced here: 1540 us
  waiting for transfers between devices  842 us (54%)
  matrix products  276 us (18%)
  blocking collectives  167 us (11%)
  local copies, waits for them, and re-layouts  165 us (11%)
  other arithmetic  69.2 us (4%)
  between operations  16.5 us (1%)
    psum x1, waiting for transfers between devices, body(): lax.psum(shards[1].astype(jnp.bfloat16), 'tile').astype(jnp.float32)  144 us
    reduce_scatter x1, waiting for transfers between devices, body(): lax.psum_scatter(grad_frame_keys.astype(jnp.bfloat16), 'tile', scatter_di...  122 us
    all_gather x1, blocking collectives, body(): lax.all_gather(expand_bias, 'seq', axis=0, tiled=True)  95.4 us
    reduce_scatter x1, waiting for transfers between devices, body(): lax.psum_scatter(local_grads[5].astype(jnp.bfloat16), 'seq', scatter_dime...  75.2 us
    reduce_scatter x1, waiting for transfers between devices, body(): lax.psum_scatter(local_grads[6].astype(jnp.bfloat16), 'seq', scatter_dime...  74.6 us
    reduce_scatter x1, waiting for transfers between devices, body(): lax.psum_scatter(local_grads[1].astype(jnp.bfloat16), 'seq', scatter_dime...  65.4 us
    reduce_scatter x1, waiting for transfers between devices, body(): lax.psum_scatter(local_grads[3].astype(jnp.bfloat16), 'seq', scatter_dime...  65 us
    unnamed x22, waiting for transfers between devices  60.8 us
  transfers between devices with their start and end apart: 22, of which 17 were waited for; matrix products, arithmetic and copies ran while one was open for 20% of the time, Pallas kernels for 0%

profile of v1, /device:TPU:0, one launch (start us, length us, event | category | flops | bytes accessed | tf_op | source)
XLA Modules:
  0.0 1542.4 jit_solution(11276677049070969725)
XLA Ops:
  8.0 10.5 all_gather.36
  23.7 8.9 all_gather.38
  42.3 15.9 %all-gather.10.cloned.1.call-done = bf16[1024,3072]{1,0:T(8,128)(2,1)} async-done(((bf16[128,3072]{1,0:T(8,128)(2,1)}), bf16[1024,3072]{1,0:T(8,128)(2,1)}) %all-gather.10.cloned.1.call-update) | async-done | bytes 6291472 | tf_op jit(solution)/shard_map/all_gather | solution.py:94
  58.2 8.0 convolution_convert_fusion.6
  72.1 12.3 collective-permute-done
  88.3 46.5 %collective-permute-done.1 = bf16[1024,1024]{1,0:T(8,128)(2,1)S(1)} collective-permute-done((bf16[1024,1024]{1,0:T(8,128)(2,1)}, bf16[1024,1024]{1,0:T(8,128)(2,1)S(1)}, u32[]{:S(2)}, u32[]{:S(2)}) %collective-permute-start.1) | collective-permute-done | bytes 2097184 | tf_op jit(solution)/shard_map/ppermute | solution.py:71
  140.6 95.4 %all-gather = bf16[8,1,512]{2,1,0:T(2,128)(2,1)S(1)} all-gather(bf16[1,1,512]{2,1,0:T(2,128)(2,1)S(1)} %reshape.516), channel_id=1, replica_groups=mesh['seq'=8,'tile'=4] {'seq'}, dimensions={0}, use_global_device_ids=true | all-gather | bytes 9216 | tf_op jit(solution)/shard_map/all_gather | solution.py:100
  258.5 10.3 copy.60
  268.8 48.4 %all-gather.14.cloned.1.call-done = bf16[1,13,256,1024]{3,2,1,0:T(8,128)(2,1)} async-done(((bf16[1,13,64,1024]{3,2,1,0:T(8,128)(2,1)}), bf16[1,13,256,1024]{3,2,1,0:T(8,128)(2,1)}) %all-gather.14.cloned.1.call-update) | async-done | bytes 6815760 | tf_op jit(solution)/shard_map/all_gather | solution.py:131
  317.1 10.3 copy.61
  339.5 8.1 convert_bitcast_fusion.2
  366.1 26.2 %all-gather.18.cloned.1.call-done = bf16[1024,3072]{1,0:T(8,128)(2,1)} async-done(((bf16[128,3072]{1,0:T(8,128)(2,1)}), bf16[1024,3072]{1,0:T(8,128)(2,1)}) %all-gather.18.cloned.1.call-update) | async-done | bytes 6291472 | tf_op jit(solution)/shard_map/all_gather | solution.py:96
  392.3 10.5 convolution_convert_fusion.5
  402.8 13.3 reshape.501
  449.6 28.7 %all-gather.22.cloned.1.call-done = bf16[1024,4096]{1,0:T(8,128)(2,1)} async-done(((bf16[128,4096]{1,0:T(8,128)(2,1)}), bf16[1024,4096]{1,0:T(8,128)(2,1)}) %all-gather.22.cloned.1.call-update) | async-done | bytes 8388624 | tf_op jit(solution)/shard_map/all_gather | solution.py:98
  478.3 14.1 fusion.64
  492.4 25.0 %fusion.72 = (bf16[4096]{0:T(1024)(128)(2,1)}, bf16[832,4096]{1,0:T(8,128)(2,1)}) fusion(f32[832,4096]{1,0:T(8,128)} %fusion.64, f32[4096]{0:T(1024)S(1)} %bitcast.187, bf16[832,1024]{1,0:T(8,128)(2,1)S(1)} %bitcast.166, bf16[8192,1024]{1,0:T(8,128)(2,1)} %copy-done.39, s32[]{:T(128)S(6)} %select_n.21), kind=kOutput, calls=%fused_computation.156 | convolution fusion | flops 7054290944 | bytes 30564356 | tf_op jit(solution)/shard_map/rd,fd->rf/dot_general | solution.py:190
  517.4 11.4 multiply_reduce_fusion.3
  539.7 9.0 convert_bitcast_fusion
  548.8 11.9 multiply_reduce_fusion.2
  560.7 8.1 multiply_convert_fusion.5
  584.3 13.8 convert_element_type.256
  598.2 10.2 multiply_reduce_fusion.4
  622.5 8.1 convolution_convert_fusion.2
  630.6 10.2 copy.78
  640.9 13.3 multiply_reduce_fusion
  654.2 10.4 multiply_convert_fusion.1
  669.6 10.3 copy.76
  693.7 11.5 convolution_convert_fusion.3
  707.2 14.4 convolution_convert_fusion.1
  723.0 17.0 %convolution_convert_fusion = bf16[4096,1024]{1,0:T(8,128)(2,1)} fusion(bf16[832,1024]{1,0:T(8,128)(2,1)S(1)} %bitcast.167, f32[832,4096]{1,0:T(8,128)} %fusion.64, f32[4096]{0:T(1024)S(1)} %bitcast.188), kind=kOutput, calls=%fused_computation.33 | convolution fusion | flops 7017594880 | bytes 23740416 | tf_op jit(solution)/shard_map/rf,rd->fd/dot_general | solution.py:189
  740.1 8.8 fusion.35
  760.2 122.1 %reduce-scatter.18.cloned.1.call-done = bf16[1,13,64,1024]{3,2,1,0:T(8,128)(2,1)} async-done(((bf16[1,13,256,1024]{3,2,1,0:T(8,128)(2,1)}), bf16[1,13,64,1024]{3,2,1,0:T(8,128)(2,1)}) %reduce-scatter.18.cloned.1.call-update) | async-done | bytes 1703952 | tf_op jit(solution)/shard_map/reduce_scatter | solution.py:258
  882.3 11.4 convolution_convert_fusion.4
  895.9 12.4 multiply_reduce_fusion.5
  919.1 8.7 reduce-scatter.24.cloned.1.call-done
  927.8 45.5 %reduce-scatter.28.cloned.1.call-done = bf16[128,1024]{1,0:T(8,128)(2,1)} async-done(((bf16[1024,1024]{1,0:T(8,128)(2,1)}), bf16[128,1024]{1,0:T(8,128)(2,1)}) %reduce-scatter.28.cloned.1.call-update) | async-done | bytes 262160 | tf_op jit(solution)/shard_map/reduce_scatter | solution.py:312
  973.3 65.0 %reduce-scatter.26.cloned.1.call-done = bf16[128,3072]{1,0:T(8,128)(2,1)} async-done(((bf16[1024,3072]{1,0:T(8,128)(2,1)}), bf16[128,3072]{1,0:T(8,128)(2,1)}) %reduce-scatter.26.cloned.1.call-update) | async-done | bytes 786448 | tf_op jit(solution)/shard_map/reduce_scatter | solution.py:309
  1038.3 75.2 %reduce-scatter.30.cloned.1.call-done = bf16[128,4096]{1,0:T(8,128)(2,1)} async-done(((bf16[1024,4096]{1,0:T(8,128)(2,1)}), bf16[128,4096]{1,0:T(8,128)(2,1)}) %reduce-scatter.30.cloned.1.call-update) | async-done | bytes 1048592 | tf_op jit(solution)/shard_map/reduce_scatter | solution.py:315
  1113.5 74.6 %reduce-scatter.32.cloned.1.call-done = bf16[512,1024]{1,0:T(8,128)(2,1)} async-done(((bf16[4096,1024]{1,0:T(8,128)(2,1)}), bf16[512,1024]{1,0:T(8,128)(2,1)}) %reduce-scatter.32.cloned.1.call-update) | async-done | bytes 1048592 | tf_op jit(solution)/shard_map/reduce_scatter | solution.py:318
  1188.1 65.4 %reduce-scatter.22.cloned.1.call-done = bf16[128,3072]{1,0:T(8,128)(2,1)} async-done(((bf16[1024,3072]{1,0:T(8,128)(2,1)}), bf16[128,3072]{1,0:T(8,128)(2,1)}) %reduce-scatter.22.cloned.1.call-update) | async-done | bytes 786448 | tf_op jit(solution)/shard_map/reduce_scatter | solution.py:303
  1253.5 8.7 all-gather.1
  1265.8 24.0 %all-reduce.2 = (bf16[4096]{0:T(1024)(128)(2,1)S(1)}, bf16[1024]{0:T(1024)(128)(2,1)S(1)}) all-reduce(bf16[4096]{0:T(1024)(128)(2,1)S(1)} %copy-done.54, bf16[1024]{0:T(1024)(128)(2,1)S(1)} %reduce_sum.249), channel_id=11, replica_groups=mesh['seq'=8,'tile'=4] {'seq'}, use_global_device_ids=true, to_apply=%region_36.37.clone | all-reduce | flops 5120 | bytes 20480
  1290.0 15.2 add_convert_fusion
  1306.0 21.9 %reduce-scatter.38.cloned.1.call-done = bf16[128,3]{1,0:T(8,128)(2,1)} async-done(((bf16[1024,3]{1,0:T(8,128)(2,1)}), bf16[128,3]{1,0:T(8,128)(2,1)}) %reduce-scatter.38.cloned.1.call-update) | async-done | bytes 784
  1328.7 36.3 %reduce-scatter.34.cloned.1.call-done = bf16[128,8]{1,0:T(8,128)(2,1)} async-done(((bf16[1024,8]{1,0:T(8,128)(2,1)}), bf16[128,8]{1,0:T(8,128)(2,1)}) %reduce-scatter.34.cloned.1.call-update) | async-done | bytes 2064
  1365.8 11.9 all-reduce.3
  1380.5 144.3 %all-reduce.7.cloned.1.call-done = (bf16[128,3072]{1,0:T(8,128)(2,1)}, bf16[128,1024]{1,0:T(8,128)(2,1)}, bf16[128,3072]{1,0:T(8,128)(2,1)}, bf16[128,1024]{1,0:...) async-done(((bf16[128,3072]{1,0:T(8,128)(2,1)}, bf16[128,1024]{1,0:T(8,128)(2,1)}, bf16[128,3072]{1,0:T(8,128)(2,1)}, bf16[128,1024]{1,0:T(8,128)(2,1)}, ...) | async-done | bytes 4194320 | tf_op jit(solution)/shard_map/psum | solution.py:336
  (293 shorter events, 222.4 us)
Async XLA Ops:
  7.2 16.5 %copy-start.63 = (bf16[3,128]{1,0:T(4,128)(2,1)S(1)}, bf16[3,128]{1,0:T(4,128)(2,1)}, u32[]{:S(2)}) copy-start(bf16[3,128]{1,0:T(4,128)(2,1)} %param.29) | copy-start | bytes 2308
  7.2 25.4 %copy-start.64 = (bf16[3,128]{1,0:T(4,128)(2,1)S(1)}, bf16[3,128]{1,0:T(4,128)(2,1)}, u32[]{:S(2)}) copy-start(bf16[3,128]{1,0:T(4,128)(2,1)} %param.28) | copy-start | bytes 2308
  7.2 51.0 %all-gather.10.cloned.1.call-start = ((), (), s32[]{:S(2)}) async-start(), calls=%async_computation.11 | async-start | bytes 7077888 | tf_op jit(solution)/shard_map/all_gather | solution.py:94
  7.9 250.6 %all-gather.12.cloned.1.call-start = ((), (), s32[]{:S(2)}) async-start(), calls=%async_computation.12 | async-start | bytes 8519680 | tf_op jit(solution)/shard_map/all_gather | solution.py:132
  21.5 20.9 %copy-start.42 = (f32[832]{0:T(1024)}, f32[832]{0:T(1024)S(1)}, u32[]{:S(2)}) copy-start(f32[832]{0:T(1024)S(1)} %div.57) | copy-start | bytes 9988
  23.6 42.7 %copy-start.4 = (f32[1,13,64,1024]{3,2,1,0:T(8,128)}, f32[1,13,64,1024]{3,2,1,0:T(8,128)S(1)}, u32[]{:S(2)}) copy-start(f32[1,13,64,1024]{3,2,1,0:T(8,128)S(1)} %get-tuple-element.47) | copy-start | bytes 10223620
  23.7 42.6 %copy-start.44 = (f32[832]{0:T(1024)}, f32[832]{0:T(1024)S(1)}, u32[]{:S(2)}) copy-start(f32[832]{0:T(1024)S(1)} %rsqrt.28) | copy-start | bytes 9988
  40.5 351.8 %copy-start.57 = (f32[1,1024]{1,0:T(1,128)}, f32[1,1024]{1,0:T(1,128)S(1)}, u32[]{:S(2)}) copy-start(f32[1,1024]{1,0:T(1,128)S(1)} %get-tuple-element.52) | copy-start | bytes 12292
  40.5 437.8 %copy-start.55 = (f32[1,1024]{1,0:T(1,128)}, f32[1,1024]{1,0:T(1,128)S(1)}, u32[]{:S(2)}) copy-start(f32[1,1024]{1,0:T(1,128)S(1)} %get-tuple-element.51) | copy-start | bytes 12292
  40.5 25.8 %copy-start.46 = (f32[1,1024]{1,0:T(1,128)}, f32[1,1024]{1,0:T(1,128)S(1)}, u32[]{:S(2)}) copy-start(f32[1,1024]{1,0:T(1,128)S(1)} %get-tuple-element.50) | copy-start | bytes 12292
  40.5 351.8 %copy-start.50 = (f32[1,1024]{1,0:T(1,128)}, f32[1,1024]{1,0:T(1,128)S(1)}, u32[]{:S(2)}) copy-start(f32[1,1024]{1,0:T(1,128)S(1)} %get-tuple-element.49) | copy-start | bytes 12292
  68.8 248.4 %all-gather.14.cloned.1.call-start = ((), (), s32[]{:S(2)}) async-start(), calls=%async_computation.13 | async-start | bytes 8519680 | tf_op jit(solution)/shard_map/all_gather | solution.py:131
  69.5 290.2 %all-gather.16.cloned.1.call-start = ((), (), s32[]{:S(2)}) async-start(), calls=%async_computation.14 | async-start | bytes 2359296 | tf_op jit(solution)/shard_map/all_gather | solution.py:95
  70.1 322.2 %all-gather.18.cloned.1.call-start = ((), (), s32[]{:S(2)}) async-start(), calls=%async_computation.15 | async-start | bytes 7077888 | tf_op jit(solution)/shard_map/all_gather | solution.py:96
  70.7 371.9 %all-gather.20.cloned.1.call-start = ((), (), s32[]{:S(2)}) async-start(), calls=%async_computation.16 | async-start | bytes 2359296 | tf_op jit(solution)/shard_map/all_gather | solution.py:97
  70.7 13.7 collective-permute-start
  87.0 47.8 %collective-permute-start.1 = (bf16[1024,1024]{1,0:T(8,128)(2,1)}, bf16[1024,1024]{1,0:T(8,128)(2,1)S(1)}, u32[]{:S(2)}, u32[]{:S(2)}) collective-permute-start(bf16[1024,1024]{1,0:T(8,128)(2,1)} %pad_maximum_fusion.3), channel_id=1, source_target_pairs={{0,24},{4,28},{8,0},{12,4},{16,8},{20,12},{24,16},{28,20},{1,25},{... | collective-permute-start | bytes 6291464 | tf_op jit(solution)/shard_map/ppermute | solution.py:71
  88.2 52.3 %copy-start.65 = (bf16[512]{0:T(512)(128)(2,1)S(1)}, bf16[512]{0:T(512)(128)(2,1)}, u32[]{:S(2)}) copy-start(bf16[512]{0:T(512)(128)(2,1)} %param.26) | copy-start | bytes 3076
  88.3 147.8 %copy-start.62 = (s32[1,13]{1,0:T(1,128)S(1)}, s32[1,13]{1,0:T(1,128)}, u32[]{:S(2)}) copy-start(s32[1,13]{1,0:T(1,128)} %param.17) | copy-start | bytes 160
  88.3 390.0 %all-gather.22.cloned.1.call-start = ((), (), s32[]{:S(2)}) async-start(), calls=%async_computation.17 | async-start | bytes 9437184 | tf_op jit(solution)/shard_map/all_gather | solution.py:98
  138.1 99.5 %collective-permute-start.2 = (bf16[2048,1024]{1,0:T(8,128)(2,1)}, bf16[2048,1024]{1,0:T(8,128)(2,1)}, u32[]{:S(2)}, u32[]{:S(2)}) collective-permute-start(bf16[2048,1024]{1,0:T(8,128)(2,1)} %pad_maximum_fusion.2), channel_id=1, source_target_pairs={{0,16},{4,20},{8,24},{12,28},{16,0},{20,4},{24,8},{28,12},{1,17},{... | collective-permute-start | bytes 12582920 | tf_op jit(solution)/shard_map/ppermute | solution.py:71
  140.5 619.7 %reduce-scatter.20.cloned.1.call-start = ((), (), s32[]{:S(2)}) async-start(), calls=%async_computation.19 | async-start | bytes 8519680 | tf_op jit(solution)/shard_map/reduce_scatter | solution.py:261
  236.0 256.4 %copy-start.52 = (f32[8,1,512]{2,1,0:T(1,128)}, f32[8,1,512]{2,1,0:T(1,128)S(1)}, u32[]{:S(2)}) copy-start(f32[8,1,512]{2,1,0:T(1,128)S(1)} %convert_element_type.288) | copy-start | bytes 49156
  363.8 39.0 %copy-start.40 = (f32[832]{0:T(1024)}, f32[832]{0:T(1024)S(1)}, u32[]{:S(2)}) copy-start(f32[832]{0:T(1024)S(1)} %broadcast_multiply_fusion.8) | copy-start | bytes 9988
  366.0 36.8 %copy-start.48 = (f32[832]{0:T(1024)}, f32[832]{0:T(1024)S(1)}, u32[]{:S(2)}) copy-start(f32[832]{0:T(1024)S(1)} %add_rsqrt_fusion.2) | copy-start | bytes 9988
  447.8 81.1 %copy-start.18 = (f32[832,1024]{1,0:T(8,128)}, f32[832,1024]{1,0:T(8,128)S(1)}, u32[]{:S(2)}) copy-start(f32[832,1024]{1,0:T(8,128)S(1)} %get-tuple-element.61) | copy-start | bytes 10223620
  478.3 14.1 copy-start.26
  478.3 39.1 %slice-start = ((s8[8388608]{0:T(1024)(128)(4,1)}), s8[4194304]{0:T(1024)(128)(4,1)S(1)}, s32[]{:S(2)}) async-start(s8[8388608]{0:T(1024)(128)(4,1)} %bitcast.199), calls=%async_computation.30 | async-start | bytes 8388608
  492.4 25.0 %slice-start.1 = ((s8[8388608]{0:T(1024)(128)(4,1)}), s8[4194304]{0:T(1024)(128)(4,1)S(1)}, s32[]{:S(2)}) async-start(s8[8388608]{0:T(1024)(128)(4,1)} %bitcast.199), calls=%async_computation.31 | async-start | bytes 8388608
  584.3 13.8 copy-start.22
  584.3 13.8 copy-start.41
  584.3 13.8 copy-start.49
  584.3 13.8 copy-start.51
  640.8 241.5 %reduce-scatter.18.cloned.1.call-start = ((), (), s32[]{:S(2)}) async-start(), calls=%async_computation.18 | async-start | bytes 8519680 | tf_op jit(solution)/shard_map/reduce_scatter | solution.py:258
  679.9 247.9 %reduce-scatter.24.cloned.1.call-start = ((), (), s32[]{:S(2)}) async-start(), calls=%async_computation.21 | async-start | bytes 2359296 | tf_op jit(solution)/shard_map/reduce_scatter | solution.py:306
  687.0 286.3 %reduce-scatter.28.cloned.1.call-start = ((), (), s32[]{:S(2)}) async-start(), calls=%async_computation.23 | async-start | bytes 2359296 | tf_op jit(solution)/shard_map/reduce_scatter | solution.py:312
  693.7 344.6 %reduce-scatter.26.cloned.1.call-start = ((), (), s32[]{:S(2)}) async-start(), calls=%async_computation.22 | async-start | bytes 7077888 | tf_op jit(solution)/shard_map/reduce_scatter | solution.py:309
  705.2 408.3 %reduce-scatter.30.cloned.1.call-start = ((), (), s32[]{:S(2)}) async-start(), calls=%async_computation.24 | async-start | bytes 9437184 | tf_op jit(solution)/shard_map/reduce_scatter | solution.py:315
  721.6 466.5 %reduce-scatter.32.cloned.1.call-start = ((), (), s32[]{:S(2)}) async-start(), calls=%async_computation.25 | async-start | bytes 9437184 | tf_op jit(solution)/shard_map/reduce_scatter | solution.py:318
  740.1 513.4 %reduce-scatter.22.cloned.1.call-start = ((), (), s32[]{:S(2)}) async-start(), calls=%async_computation.20 | async-start | bytes 7077888 | tf_op jit(solution)/shard_map/reduce_scatter | solution.py:303
  893.8 411.4 %reduce-scatter.36.cloned.1.call-start = ((), (), s32[]{:S(2)}) async-start(), calls=%async_computation.27 | async-start | bytes 294912
  909.3 418.6 %reduce-scatter.38.cloned.1.call-start = ((), (), s32[]{:S(2)}) async-start(), calls=%async_computation.28 | async-start | bytes 294912
  915.4 338.1 %copy-start.66 = (bf16[128]{0:T(256)(128)(2,1)S(1)}, bf16[128]{0:T(256)(128)(2,1)}, u32[]{:S(2)}) copy-start(bf16[128]{0:T(256)(128)(2,1)} %param.27) | copy-start | bytes 772
  917.8 346.1 %copy-start.69 = (u32[32]{0:T(128)S(1)}, u32[32]{0:T(128)}, u32[]{:S(2)}) copy-start(u32[32]{0:T(128)} %constant.78) | copy-start | bytes 388
  917.8 348.0 %copy-start.54 = (bf16[4096]{0:T(1024)(128)(2,1)S(1)}, bf16[4096]{0:T(1024)(128)(2,1)}, u32[]{:S(2)}) copy-start(bf16[4096]{0:T(1024)(128)(2,1)} %get-tuple-element.69) | copy-start | bytes 24580
  917.8 372.2 %copy-start.20 = (f32[832,1024]{1,0:T(8,128)S(1)}, f32[832,1024]{1,0:T(8,128)}, u32[]{:S(2)}) copy-start(f32[832,1024]{1,0:T(8,128)} %copy-done.18) | copy-start | bytes 10223620
  917.9 447.1 %reduce-scatter.34.cloned.1.call-start = ((), (), s32[]{:S(2)}) async-start(), calls=%async_computation.26 | async-start | bytes 294912
  919.1 605.8 %all-reduce.7.cloned.1.call-start = ((), (), s32[]{:S(2)}) async-start(), calls=%async_computation.29 | async-start | bytes 8388608 | tf_op jit(solution)/shard_map/psum | solution.py:336
  (46 other events, 197.6 us)
Sparse Core Ops, SparseCore 0:
  9.9 48.2 all-gather.9
  68.9 123.9 all-gather.11
  195.0 122.0 all-gather.13
  318.9 26.0 all-gather.15
  346.7 45.5 all-gather.17
  394.0 27.8 all-gather.19
  423.8 54.3 all-gather.21
  641.0 119.2 reduce-scatter.19
  762.6 119.7 reduce-scatter.17
  886.0 41.7 reduce-scatter.23
  932.0 41.2 reduce-scatter.27
  976.5 61.7 reduce-scatter.25
  1042.2 71.2 reduce-scatter.29
  1116.8 71.2 reduce-scatter.31
  1191.7 61.7 reduce-scatter.21
  1256.9 33.5 reduce-scatter.35
  1294.3 33.5 reduce-scatter.37
  1331.3 33.5 reduce-scatter.33
  1368.0 156.7 all-reduce.6
